TPU v7x, 32 devices: a whole 2x2x4 slice. The times are simulated.
32 devices in a mesh: gx: 8 (over y, x, core), gy: 4 (over z).
Axes of the slice: x: 2, y: 2, z: 4, core: 2. Of those that a mesh axis runs over, the one named last changes fastest.
Arguments:
- states: bfloat16 [512, 2048], P('gx'), may hold values from -6 to 6
- attn_gain: bfloat16 [2048], replicated, may hold values from 0.099609375 to 1.8984375
- w_qkv: bfloat16 [2048, 5120], P(None, 'gy'), may hold values from -0.125 to 0.125
- q_gain: bfloat16 [128], replicated, may hold values from 0.099609375 to 1.8984375
- k_gain: bfloat16 [128], replicated, may hold values from 0.099609375 to 1.8984375
- cache_k: bfloat16 [8, 4096, 512], P('gx', 'gy'), may hold values from -400 to 400
- cache_v: bfloat16 [8, 4096, 512], P('gx', 'gy'), may hold values from -6 to 6
- cache_len: int32 [8], P('gx'), may hold values from 256 to 4096, as said below
- tree_mask: int32 [8, 64, 64], P('gx'), may hold values from 0 to 1, as said below
- w_o: bfloat16 [4096, 2048], P(None, 'gy'), may hold values from -0.09375 to 0.09375
- ffn_gain: bfloat16 [2048], P('gy'), may hold values from 0.099609375 to 1.8984375
- routing: int32 [512, 8], replicated, may hold values from 0 to 63, all different within a row; in each aligned block of 64 rows (0 to 63, 64 to 127, ...) at most 12 rows name the same one
- route_weight: float32 [512, 8], replicated, may hold values from 0.05 to 0.5
- w_in: bfloat16 [64, 2048, 1536], P('gx', 'gy'), may hold values from -0.125 to 0.125
- w_down: bfloat16 [64, 768, 2048], P('gx', None, 'gy'), may hold values from -0.21875 to 0.21875
- accept: int32 [8, 8, 64], P('gx'), may hold values from 0 to 1, as said below
Outputs:
- layer_out: bfloat16 [512, 2048], P('gx', 'gy')
- accepted_kv: bfloat16 [8, 8, 1024], P('gx')
Inputs may be any that keep to these rules, and one draw needn't show every extreme that they name: `cache_len`: each request's cache holds keys at positions below its length; some request fills all 4096 positions. tree_mask[r, t, u] is 1 exactly when draft token u is t or an ancestor of t in request r's tree; every token's parent has a lower index and token 0 is the root. Row a of accept[r] is the one-hot of the token at depth a on one path from the root of request r's tree; the path is longer than 8 tokens. `routing`: each row names 8 different experts; in each aligned block of 64 rows no expert is named by more than 12 rows.
All inputs are finite; a program needn't handle non-finite values.
Results may differ from a plain program's by a relative error of at most 0.014.
Values may be sent and summed in bfloat16 or wider, within the bound.
A program may use at most 128 MiB of HBM per device.

v0:
```python
import math
import jax
import jax.numpy as jnp
from jax import lax
from jax.sharding import PartitionSpec as P

EPS = 1e-06
NEG = -1e30
THETA_LOG = math.log(1000000.0)


def combined_all(shard, axis, join):
    gathered = jax.tree.map(
        lambda a, kind: lax.all_gather(a.astype(kind), axis),
        shard,
        (jnp.bfloat16, jnp.bfloat16, jnp.bfloat16),
    )

    def take(source):
        return jax.tree.map(
            lambda a, own: lax.dynamic_index_in_dim(a, source, 0, False).astype(own.dtype),
            gathered,
            shard,
        )

    return lax.fori_loop(
        1, lax.axis_size(axis), lambda source, state: join(state, take(source)), take(0)
    )


def rms_scale(values, gain):
    return values * lax.rsqrt(jnp.mean(values * values, -1, keepdims=True) + EPS) * gain


def rotate(values, position):
    half = values.shape[-1] // 2
    freqs = jnp.exp(jnp.arange(half, dtype=jnp.float32) * (-2.0 * THETA_LOG / values.shape[-1]))
    angles = position.astype(jnp.float32)[..., None] * freqs
    cosine = jnp.cos(angles)
    sine = jnp.sin(angles)
    lower = values[..., :half]
    upper = values[..., half:]
    return jnp.concatenate([lower * cosine - upper * sine, upper * cosine + lower * sine], -1)


def combine_parts(earlier, later):
    max_one, sum_one, acc_one = earlier
    max_two, sum_two, acc_two = later
    joined = jnp.maximum(max_one, max_two)
    factor_one = jnp.exp(max_one - joined)
    factor_two = jnp.exp(max_two - joined)
    return (
        joined,
        sum_one * factor_one + sum_two * factor_two,
        acc_one * factor_one[..., None] + acc_two * factor_two[..., None],
    )


def body(
    states,
    attn_gain,
    w_qkv,
    q_gain,
    k_gain,
    cache_k,
    cache_v,
    cache_len,
    tree_mask,
    w_o,
    ffn_gain,
    routing,
    route_weight,
    w_in,
    w_down,
    accept,
):
    tok_rows, model_width = states.shape
    head_dim = q_gain.shape[0]
    kv_cols = cache_k.shape[2]
    kv_heads = kv_cols // head_dim
    heads_all = w_o.shape[0] // head_dim
    group = heads_all // kv_heads
    requests_here, tree_size = (tree_mask.shape[0], tree_mask.shape[1])
    cache_span = cache_k.shape[1]
    cols_here = w_o.shape[1]
    col_index = lax.axis_index("gy")
    row_index = lax.axis_index("gx")
    count_gx = lax.axis_size("gx")
    normed = rms_scale(states.astype(jnp.float32), attn_gain.astype(jnp.float32)).astype(
        jnp.bfloat16
    )
    qkv_part = jnp.dot(normed, w_qkv, preferred_element_type=jnp.float32).astype(jnp.bfloat16)
    qkv_whole = lax.all_gather(qkv_part, "gy", axis=1, tiled=True)
    q_cols = heads_all * head_dim
    query = qkv_whole[:, :q_cols].reshape(requests_here, tree_size, kv_heads, group, head_dim)
    keys_new = qkv_whole[:, q_cols : q_cols + kv_cols].reshape(
        requests_here, tree_size, kv_heads, head_dim
    )
    values_new = qkv_whole[:, q_cols + kv_cols :].reshape(
        requests_here, tree_size, kv_heads, head_dim
    )
    depth = jnp.sum(tree_mask, -1) - 1
    position = cache_len[:, None] + depth
    q_rot = rotate(
        rms_scale(query.astype(jnp.float32), q_gain.astype(jnp.float32)), position[:, :, None, None]
    ).astype(jnp.bfloat16)
    k_rot = rotate(
        rms_scale(keys_new.astype(jnp.float32), k_gain.astype(jnp.float32)), position[:, :, None]
    ).astype(jnp.bfloat16)
    cached_keys = cache_k.reshape(requests_here, cache_span, kv_heads, head_dim)
    cached_values = cache_v.reshape(requests_here, cache_span, kv_heads, head_dim)
    score_scale = head_dim ** (-0.5)
    scores_cache = (
        jnp.einsum("rtkgd,rskd->rtkgs", q_rot, cached_keys, preferred_element_type=jnp.float32)
        * score_scale
    )
    scores_tree = (
        jnp.einsum("rtkgd,rukd->rtkgu", q_rot, k_rot, preferred_element_type=jnp.float32)
        * score_scale
    )
    cache_pos = col_index * cache_span + jnp.arange(cache_span, dtype=jnp.int32)
    valid = (cache_pos[None, :] < cache_len[:, None])[:, None, None, None, :]
    tree_ok = ((tree_mask == 1) & (col_index == 0))[:, :, None, None, :]
    scores_cache = jnp.where(valid, scores_cache, NEG)
    scores_tree = jnp.where(tree_ok, scores_tree, NEG)
    row_max = jnp.maximum(jnp.max(scores_cache, -1), jnp.max(scores_tree, -1))
    probs_cache = jnp.where(valid, jnp.exp(scores_cache - row_max[..., None]), 0.0).astype(
        jnp.bfloat16
    )
    probs_tree = jnp.where(tree_ok, jnp.exp(scores_tree - row_max[..., None]), 0.0).astype(
        jnp.bfloat16
    )
    denom_sum = jnp.sum(probs_cache.astype(jnp.float32), -1) + jnp.sum(
        probs_tree.astype(jnp.float32), -1
    )
    weighted = jnp.einsum(
        "rtkgs,rskd->rtkgd", probs_cache, cached_values, preferred_element_type=jnp.float32
    )
    weighted = weighted + jnp.einsum(
        "rtkgu,rukd->rtkgd", probs_tree, values_new, preferred_element_type=jnp.float32
    )
    row_max, denom_sum, weighted = combined_all((row_max, denom_sum, weighted), "gy", combine_parts)
    attn = (weighted / denom_sum[..., None]).astype(jnp.bfloat16).reshape(tok_rows, q_cols)
    states_here = lax.dynamic_slice_in_dim(states, col_index * cols_here, cols_here, 1)
    resid = (
        states_here.astype(jnp.float32) + jnp.dot(attn, w_o, preferred_element_type=jnp.float32)
    ).astype(jnp.bfloat16)
    exp_here = w_in.shape[0]
    expert_count = exp_here * count_gx
    top_k = routing.shape[1]
    most_rows = 3 * tok_rows * top_k // (2 * expert_count)
    hidden_units = w_down.shape[1]
    gain_float = ffn_gain.astype(jnp.float32)
    own_route = lax.dynamic_slice_in_dim(routing, row_index * tok_rows, tok_rows, 0)
    own_weight = lax.dynamic_slice_in_dim(route_weight, row_index * tok_rows, tok_rows, 0)
    matched = own_route[:, :, None] == jnp.arange(expert_count, dtype=jnp.int32)[None, None, :]
    hit_count = jnp.any(matched, 1).astype(jnp.int32)
    weight_table = jnp.sum(jnp.where(matched, own_weight[:, :, None], 0.0), 1)
    slot_rank = jnp.cumsum(hit_count, 0) - 1
    slot_ids = jnp.where(
        hit_count > 0,
        jnp.arange(expert_count, dtype=jnp.int32)[None, :] * most_rows + slot_rank,
        expert_count * most_rows,
    )
    token_ids = jnp.broadcast_to(jnp.arange(tok_rows, dtype=jnp.int32)[:, None], slot_ids.shape)
    slot_table = (
        jnp.full((expert_count * most_rows,), tok_rows, jnp.int32)
        .at[slot_ids]
        .set(token_ids, mode="drop")
    )
    padded = jnp.concatenate([resid, jnp.zeros((1, cols_here), jnp.bfloat16)], 0)
    outgoing = padded[slot_table].reshape(expert_count, most_rows, cols_here)
    arrived = lax.all_to_all(outgoing, "gx", split_axis=0, concat_axis=1, tiled=True)
    arrived_float = arrived.astype(jnp.float32)
    squares = jnp.sum(arrived_float * arrived_float, -1)
    scaled = (arrived_float * gain_float).astype(jnp.bfloat16)
    partial_value = jnp.einsum("esd,edf->esf", scaled, w_in, preferred_element_type=jnp.float32)
    summed, squares = (
        lax.psum_scatter(
            partial_value.astype(jnp.bfloat16), "gy", scatter_dimension=1, tiled=True
        ).astype(jnp.float32),
        lax.psum_scatter(
            squares.astype(jnp.bfloat16), "gy", scatter_dimension=1, tiled=True
        ).astype(jnp.float32),
    )
    inverse = lax.rsqrt(squares / model_width + EPS)[..., None]
    hidden = (
        jax.nn.silu(summed[..., :hidden_units] * inverse) * (summed[..., hidden_units:] * inverse)
    ).astype(jnp.bfloat16)
    expert_out = jnp.einsum(
        "esf,efd->esd",
        lax.all_gather(hidden, "gy", axis=1, tiled=True),
        w_down,
        preferred_element_type=jnp.float32,
    )
    returned = lax.all_to_all(
        expert_out.astype(jnp.bfloat16), "gx", split_axis=1, concat_axis=0, tiled=True
    ).astype(expert_out.dtype)
    weight_pad = jnp.concatenate([weight_table, jnp.zeros((1, expert_count), jnp.float32)], 0)
    slot_expert = jnp.arange(expert_count * most_rows, dtype=jnp.int32) // most_rows
    slot_weight = weight_pad[slot_table, slot_expert]
    moe_total = (
        jnp.zeros((tok_rows + 1, cols_here), jnp.float32)
        .at[slot_table]
        .add(returned.reshape(-1, cols_here) * slot_weight[:, None])[:tok_rows]
    )
    layer_out = (resid.astype(jnp.float32) + moe_total).astype(jnp.bfloat16)
    kv_new = jnp.concatenate(
        [
            k_rot.reshape(requests_here, tree_size, kv_cols),
            values_new.reshape(requests_here, tree_size, kv_cols),
        ],
        -1,
    )
    accepted_kv = jnp.einsum(
        "rat,rtc->rac", accept.astype(jnp.bfloat16), kv_new, preferred_element_type=jnp.float32
    ).astype(jnp.bfloat16)
    return (layer_out, accepted_kv)


def solution(mesh):
    in_specs = (
        P("gx", None),
        P(),
        P(None, "gy"),
        P(),
        P(),
        P("gx", "gy", None),
        P("gx", "gy", None),
        P("gx"),
        P("gx", None, None),
        P(None, "gy"),
        P("gy"),
        P(),
        P(),
        P("gx", "gy", None),
        P("gx", None, "gy"),
        P("gx", None, None),
    )
    out_specs = (P("gx", "gy"), P("gx", None, None))
    return jax.shard_map(body, mesh=mesh, in_specs=in_specs, out_specs=out_specs, check_vma=False)
```

profile of v0, /device:TPU:0, one launch (start us, length us, event | category | flops | bytes accessed | tf_op | source)
XLA Modules:
  0.0 285.0 jit_solution(2547359270046433330)
XLA Ops:
  7.2 0.7 convert_element_type.348
  7.9 1.1 fusion.37
  9.1 3.7 %convolution_convert_fusion.1 = bf16[64,1280]{1,0:T(8,128)(2,1)S(1)} fusion(bf16[2048,1280]{1,0:T(8,128)(2,1)} %param.20, bf16[64,2048]{1,0:T(8,128)(2,1)} %param.18, f32[2048]{0:T(1024)S(1)} %convert_element_type.348, f32[64]{0:T(128)S(1)} %add_rsqrt_fusion.3), kind=kOutput, calls=%fused_computation.23 | convolution fusion | flops 336150528 | bytes 5677312 | tf_op jit(solution)/shard_map/dot_general | solution.py:92
  12.7 19.6 %all_gather.20 = bf16[64,5120]{1,0:T(8,128)(2,1)S(1)} all-gather(bf16[64,1280]{1,0:T(8,128)(2,1)S(1)} %convolution_convert_fusion.1), channel_id=1, replica_groups=mesh['gx'=8,'gy'=4] {'gy'}, dimensions={1}, use_global_device_ids=true | all-gather | bytes 819200 | tf_op jit(solution)/shard_map/all_gather | solution.py:93
  32.5 0.7 slice_bitcast_fusion.2
  34.0 0.4 multiply_reduce_fusion.1
  34.8 0.3 reshape.690
  35.1 0.3 fusion.32
  35.4 0.2 multiply_cosine_fusion
  35.6 0.4 fusion.40
  36.1 0.3 pad_maximum_fusion
  36.4 4.7 %fusion.6 = (f32[64,4,8]{2,0,1:T(8,128)S(1)}, f32[4,64,8,1024]{3,2,1,0:T(8,128)}) fusion(pred[1024]{0:T(1024)(128)(4,1)S(1)} %add_compare_fusion, bf16[64,4,8,128]{3,2,0,1:T(8,128)(2,1)S(1)} %pad_maximum_fusion, bf16[1024,4,128,1]{2,1,0,3:T(4,128)(2,1)S(1)} %bitcast.184), kind=kOutput, calls=%fused_computation.18 | convolution fusion | flops 543160320 | bytes 9970688 | tf_op jit(solution)/shard_map/rtkgd,rskd->rtkgs/dot_general | solution.py:114
  41.8 0.7 fusion.73
  42.6 0.3 fusion.58
  42.9 0.3 copy.246
  43.3 0.3 reshape.692
  43.6 0.3 fusion.56
  43.9 5.5 %fusion.24 = bf16[1,64,4,8,128]{4,3,1,2,0:T(8,128)(2,1)S(1)} fusion(f32[4,128,64,8]{1,3,2,0:T(8,128)S(1)} %fusion.56, bf16[1024,4,128,1]{2,1,0,3:T(4,128)(2,1)S(1)} %bitcast.189, f32[4,64,8,1024]{3,2,1,0:T(8,128)} %get-tuple-element.264, f32[64,4,8]{2,0,1:T(8,128)S(1)} %copy.215, pred[1024]{0:T(1024)(128)(4,1)S(1)} %add_compare_fusion), kind=kOutput, calls=%fused_computation.38 | convolution fusion | flops 547880960 | bytes 11019264 | tf_op jit(solution)/shard_map/rtkgs,rskd->rtkgd/dot_general | solution.py:136
  49.4 0.9 copy.222
  50.7 0.7 copy.232
  51.4 15.4 %fusion.77 = s32[64,64,1]{2,1,0:T(8,128)S(1)} fusion(s32[64,64,1]{2,1,0:T(8,128)S(1)} %copy.232), kind=kOutput, calls=%fused_computation.141 | output fusion | flops 258048 | bytes 32768 | tf_op jit(solution)/shard_map/jit(cumsum)/reduce_window_sum | solution.py:159
  66.8 1.2 fusion.9
  68.3 16.1 %all-gather = bf16[256,4,8]{2,1,0:T(4,128)(2,1)S(1)} all-gather(bf16[64,4,8]{2,1,0:T(4,128)(2,1)S(1)} %copy.214), channel_id=2, replica_groups=mesh['gx'=8,'gy'=4] {'gy'}, dimensions={0}, use_global_device_ids=true | all-gather | bytes 20480 | tf_op jit(solution)/shard_map/all_gather | solution.py:14
  84.6 4.7 %convert_reduce_fusion = f32[64,4,8]{2,0,1:T(8,128)S(1)} fusion(f32[64,4,8]{2,0,1:T(8,128)S(1)} %copy.215, f32[4,64,8,1024]{3,2,1,0:T(8,128)} %get-tuple-element.264, pred[1024]{0:T(1024)(128)(4,1)S(1)} %add_compare_fusion), kind=kLoop, calls=%fused_computation.16 | loop fusion | flops 14678016 | bytes 8406016 | tf_op jit(solution)/shard_map/reduce_sum | solution.py:133
  89.5 15.9 %all-gather.1 = bf16[256,4,8]{2,1,0:T(4,128)(2,1)S(1)} all-gather(bf16[64,4,8]{2,1,0:T(4,128)(2,1)S(1)} %copy.217), channel_id=3, replica_groups=mesh['gx'=8,'gy'=4] {'gy'}, dimensions={0}, use_global_device_ids=true | all-gather | bytes 20480 | tf_op jit(solution)/shard_map/all_gather | solution.py:14
  105.8 15.5 %scatter_custom_fusion = s32[768]{0:T(1024)S(1)} fusion(s32[4096]{0:T(1024)S(1)} %reshape.728, s32[4096]{0:T(1024)S(1)} %reshape.730, s32[]{:T(128)} %constant.123.clone.1), kind=kCustom, calls=%fused_computation.123 | custom fusion | bytes 3076 | tf_op jit(solution)/shard_map/scatter | solution.py:169
  121.3 1.2 slice_convert_fusion
  122.5 6.7 %while.19 = (s32[]{:T(128)}, f32[1,64,4,8]{1,3,2,0:T(8,128)S(1)}, f32[1,64,4,8]{1,3,2,0:T(8,128)S(1)}, f32[1,64,4,8,128]{4,3,2,1,0:T(8,128)S(1)}, bf16[4,1,64,4,...) while((s32[]{:T(128)}, f32[1,64,4,8]{1,3,2,0:T(8,128)S(1)}, ...), condition=%wide.region_9.10_spmd, body=%wide.region_8.9_spmd.sunk | while | flops 1069061 | bytes 2764955 | solution.py:26
  122.8 1.9 fusion.92
  125.1 1.9 fusion.92
  127.3 1.9 fusion.92
  129.4 0.3 divide_convert_fusion
  129.7 0.2 reshape.695
  130.0 3.0 %fusion.27 = bf16[64,512]{1,0:T(8,128)(2,1)S(1)} fusion(bf16[64,4096]{1,0:T(8,128)(2,1)S(1)} %reshape.695, bf16[4096,512]{1,0:T(8,128)(2,1)} %param.27, bf16[64,2048]{1,0:T(8,128)(2,1)} %param.18, s32[]{:T(128)S(6)} %select_n.93), kind=kOutput, calls=%fused_computation.40 | convolution fusion | flops 268533760 | bytes 4849668 | tf_op jit(solution)/shard_map/dot_general | solution.py:146
  133.0 2.7 gather_fusion
  135.7 1.2 reshape.696
  136.9 3.6 %all-to-all-start = ((bf16[64,12,512]{2,1,0:T(8,128)(2,1)}), bf16[64,12,512]{2,1,0:T(8,128)(2,1)S(1)}, u32[]{:S(2)}, u32[]{:S(2)}) async-start(bf16[64,12,512]{2,1,0:T(8,128)(2,1)} %reshape.696), calls=%async_computation | async-start | bytes 2097152 | tf_op jit(solution)/shard_map/all_to_all | solution.py:173
  140.6 15.3 %all-to-all-done = bf16[64,12,512]{2,1,0:T(8,128)(2,1)S(1)} async-done(((bf16[64,12,512]{2,1,0:T(8,128)(2,1)}), bf16[64,12,512]{2,1,0:T(8,128)(2,1)S(1)}, u32[]{:S(2)}, u32[]{:S(2)}) %all-to-all-start) | async-done | bytes 786464 | tf_op jit(solution)/shard_map/all_to_all | solution.py:173
  155.9 0.5 copy.234
  156.4 0.2 fusion.10
  156.6 6.7 %fusion.74 = bf16[12,8,8,1536]{3,1,0,2:T(8,128)(2,1)S(1)} fusion(bf16[8,512,1536]{2,1,0:T(8,128)(2,1)} %param.31, bf16[8,96,512]{2,0,1:T(8,128)(2,1)S(1)} %fusion.10), kind=kOutput, calls=%fused_computation.140 | convolution fusion | flops 1209139200 | bytes 15728640 | tf_op jit(solution)/shard_map/esd,edf->esf/dot_general | solution.py:177
  163.3 1.7 copy.265
  165.0 0.6 copy-done.10
  165.6 0.6 dynamic-slice
  166.9 0.3 multiply_reduce_fusion
  167.6 11.3 %all-reduce.2 = bf16[8,96]{1,0:T(8,128)(2,1)S(1)} all-reduce(bf16[8,96]{1,0:T(8,128)(2,1)S(1)} %convert_element_type.390), channel_id=6, replica_groups=mesh['gx'=8,'gy'=4] {'gy'}, use_global_device_ids=true, to_apply=%region_15.16.clone | all-reduce | flops 768 | bytes 3072
  179.0 32.8 %reduce-scatter.5.cloned.1.call-done = bf16[24,12288]{1,0:T(8,128)(2,1)} async-done(((bf16[96,12288]{1,0:T(8,128)(2,1)}), bf16[24,12288]{1,0:T(8,128)(2,1)}) %reduce-scatter.5.cloned.1.call-update) | async-done | bytes 589840
  211.9 1.2 copy.266
  213.1 0.2 copy_convert_fusion
  213.3 1.0 fusion.36
  214.3 30.1 %all-gather.6.cloned.1.call-done = bf16[8,96,768]{2,1,0:T(8,128)(2,1)} async-done(((bf16[8,24,768]{2,1,0:T(8,128)(2,1)}), bf16[8,96,768]{2,1,0:T(8,128)(2,1)}) %all-gather.6.cloned.1.call-update) | async-done | bytes 1179664 | tf_op jit(solution)/shard_map/all_gather | solution.py:192
  244.4 4.3 %convolution_convert_fusion.2 = bf16[8,96,512]{2,1,0:T(8,128)(2,1)S(1)} fusion(bf16[8,96,768]{2,1,0:T(8,128)(2,1)} %all-gather.6.cloned.1.call-done, bf16[8,768,512]{2,1,0:T(8,128)(2,1)} %param.32), kind=kOutput, calls=%fused_computation.31 | convolution fusion | flops 604372992 | bytes 8257536 | tf_op jit(solution)/shard_map/esf,efd->esd/dot_general | solution.py:190
  248.7 1.3 copy.238
  250.0 3.8 %all-to-all-start.1 = ((bf16[8,96,512]{2,0,1:T(8,128)(2,1)}), bf16[8,96,512]{2,0,1:T(8,128)(2,1)S(1)}, u32[]{:S(2)}, u32[]{:S(2)}) async-start(bf16[8,96,512]{2,0,1:T(8,128)(2,1)} %copy.238), calls=%async_computation.1 | async-start | bytes 1572864 | tf_op jit(solution)/shard_map/all_to_all | solution.py:196
  253.8 0.8 constant_dynamic-slice_fusion
  254.6 0.2 select_reduce_fusion
  254.9 5.1 %gather_fusion.1 = f32[768]{0:T(1024)S(1)} fusion(f32[65,64]{1,0:T(8,128)S(1)} %concatenate.45, s32[768]{0:T(1024)S(1)} %fusion.62), kind=kCustom, calls=%fused_computation.1 | custom fusion | bytes 12288 | tf_op jit(solution)/shard_map/gather | solution.py:201
  260.2 0.7 fusion.28
  260.9 5.3 %all-to-all-done.1 = bf16[8,96,512]{2,0,1:T(8,128)(2,1)S(1)} async-done(((bf16[8,96,512]{2,0,1:T(8,128)(2,1)}), bf16[8,96,512]{2,0,1:T(8,128)(2,1)S(1)}, u32[]{:S(2)}, u32[]{:S(2)}) %all-to-all-start.1) | async-done | bytes 786464 | tf_op jit(solution)/shard_map/all_to_all | solution.py:196
  266.3 0.2 convert_bitcast_fusion
  266.5 0.9 copy.239
  267.4 1.3 reshape.709
  268.8 9.0 %scatter_custom_fusion.1 = f32[65,512]{1,0:T(8,128)S(1)} fusion(s32[768]{0:T(1024)S(1)} %get-tuple-element.260, f32[768,512]{1,0:T(8,128)} %reshape.709, f32[768]{0:T(1024)S(1)} %gather_fusion.1, f32[]{:T(128)} %constant.113.clone.1), kind=kCustom, calls=%fused_computation.29 | custom fusion | flops 786432 | bytes 1710084 | tf_op jit(solution)/shard_map/scatter-add | solution.py:205
  277.8 0.6 fusion.47
  (99 shorter events, 4.6 us)
Async XLA Ops:
  7.2 43.1 %copy-start = (s32[512,8]{0,1:T(8,128)S(1)}, s32[512,8]{0,1:T(8,128)}, u32[]{:S(2)}) copy-start(s32[512,8]{0,1:T(8,128)} %param.29) | copy-start | bytes 49156
  7.2 114.2 %all-gather.8.cloned.1.call-start = ((), (), s32[]{:S(2)}) async-start(), calls=%async_computation.4 | async-start | bytes 2621440 | tf_op jit(solution)/shard_map/all_gather | solution.py:14
  12.7 21.2 %copy-start.8 = (bf16[128]{0:T(256)(128)(2,1)S(1)}, bf16[128]{0:T(256)(128)(2,1)}, u32[]{:S(2)}) copy-start(bf16[128]{0:T(256)(128)(2,1)} %param.21) | copy-start | bytes 772
  32.4 2.2 copy-start.4
  32.4 2.3 copy-start.2
  36.4 4.8 %copy-start.9 = (bf16[128]{0:T(256)(128)(2,1)S(1)}, bf16[128]{0:T(256)(128)(2,1)}, u32[]{:S(2)}) copy-start(bf16[128]{0:T(256)(128)(2,1)} %param.22) | copy-start | bytes 772
  41.8 1.4 copy-start.3
  135.7 4.8 %copy-start.6 = (bf16[512]{0:T(512)(128)(2,1)S(1)}, bf16[512]{0:T(512)(128)(2,1)}, u32[]{:S(2)}) copy-start(bf16[512]{0:T(512)(128)(2,1)} %param.28) | copy-start | bytes 3076
  136.9 19.0 %all-to-all-start = ((bf16[64,12,512]{2,1,0:T(8,128)(2,1)}), bf16[64,12,512]{2,1,0:T(8,128)(2,1)S(1)}, u32[]{:S(2)}, u32[]{:S(2)}) async-start(bf16[64,12,512]{2,1,0:T(8,128)(2,1)} %reshape.696), calls=%async_computation | async-start | bytes 2097152 | tf_op jit(solution)/shard_map/all_to_all | solution.py:173
  140.5 71.4 %reduce-scatter.5.cloned.1.call-start = ((), (), s32[]{:S(2)}) async-start(), calls=%async_computation.5 | async-start | bytes 2949120
  165.0 0.7 copy-start.10
  165.0 79.4 %all-gather.6.cloned.1.call-start = ((), (), s32[]{:S(2)}) async-start(), calls=%async_computation.3 | async-start | bytes 1474560 | tf_op jit(solution)/shard_map/all_gather | solution.py:192
  250.0 16.3 %all-to-all-start.1 = ((bf16[8,96,512]{2,0,1:T(8,128)(2,1)}), bf16[8,96,512]{2,0,1:T(8,128)(2,1)S(1)}, u32[]{:S(2)}, u32[]{:S(2)}) async-start(bf16[8,96,512]{2,0,1:T(8,128)(2,1)} %copy.238), calls=%async_computation.1 | async-start | bytes 1572864 | tf_op jit(solution)/shard_map/all_to_all | solution.py:196
  254.9 5.3 %copy-start.5 = (bf16[1,64,512]{2,1,0:T(8,128)(2,1)S(1)}, bf16[1,64,512]{2,1,0:T(8,128)(2,1)}, u32[]{:S(2)}) copy-start(bf16[1,64,512]{2,1,0:T(8,128)(2,1)} %get-tuple-element.254) | copy-start | bytes 196612
  254.9 5.3 %copy-start.7 = (s32[1,8,64]{2,1,0:T(8,128)S(1)}, s32[1,8,64]{2,1,0:T(8,128)}, u32[]{:S(2)}) copy-start(s32[1,8,64]{2,1,0:T(8,128)} %param.33) | copy-start | bytes 6148
  266.5 11.9 %copy-start.1 = (s32[512,8]{0,1:T(8,128)S(1)}, s32[512,8]{0,1:T(8,128)}, u32[]{:S(2)}) copy-start(s32[512,8]{0,1:T(8,128)} %param.29) | copy-start | bytes 49156
Sparse Core Ops, SparseCore 0:
  50.4 54.0 all-gather.7
  165.1 46.7 reduce-scatter.4
  214.4 29.9 all-gather.5
where the time goes:
time: 286 us; the launch traced here: 285 us
  waiting for transfers between devices  83.7 us (29%)
  blocking collectives  63 us (22%)
  other arithmetic  46 us (16%)
  local copies, waits for them, and re-layouts  39.4 us (14%)
  matrix products  29.6 us (10%)
  between operations  15.7 us (5%)
  starting transfers between devices  7.49 us (3%)
    unnamed x4, waiting for transfers between devices  32.9 us
    all_gather x2, blocking collectives, combined_all(): lax.all_gather(a.astype(kind), axis)  32 us
    all_gather x1, waiting for transfers between devices, body(): lax.all_gather(hidden, 'gy', axis=1, tiled=True)  30.1 us
    all_gather x1, blocking collectives, body(): qkv_whole = lax.all_gather(qkv_part, 'gy', axis=1, tiled=True)  19.6 us
    scatter x1, local copies, waits for them, and re-layouts, body(): slot_table = jnp.full((expert_count * most_rows,), tok_rows, jnp.int32).a...  15.5 us
    another operation x1, other arithmetic, body(): slot_rank = jnp.cumsum(hit_count, 0) - 1  15.4 us
    all_to_all x1, waiting for transfers between devices, body(): lax.all_to_all(outgoing, 'gx', split_axis=0, concat_axis=1, tiled=True)  15.3 us
    unnamed x1, blocking collectives  11.3 us
  transfers between devices with their start and end apart: 5, of which 4 were waited for; matrix products, arithmetic and copies ran while one was open for 17% of the time, Pallas kernels for 0%

commit v1 on v0

--- a/solution.py
+++ b/solution.py
@@ -187,11 +187,22 @@
     hidden = (
         jax.nn.silu(summed[..., :hidden_units] * inverse) * (summed[..., hidden_units:] * inverse)
     ).astype(jnp.bfloat16)
+
+    def note_islands_all(slab_in, mesh_dim):
+        how_many = lax.axis_size(mesh_dim)
+        fields = [(no, (no + 1) % how_many) for no in range(how_many)]
+        cards = [(no, (no - 1) % how_many) for no in range(how_many)]
+        block_out, kept_arr = ([slab_in], [slab_in])
+        for _ in range(how_many // 2):
+            block_out.append(lax.ppermute(block_out[-1], axis_name=mesh_dim, perm=fields))
+        for _ in tuple(range((how_many - 1) // 2)):
+            kept_arr.append(lax.ppermute(kept_arr[-1], axis_name=mesh_dim, perm=cards))
+        y1 = jnp.concatenate([*block_out[::-1], *kept_arr[1:]], 1)
+        field_out = jnp.roll(y1, (lax.axis_index(mesh_dim) - how_many // 2) * slab_in.shape[1], 1)
+        return field_out
+
     expert_out = jnp.einsum(
-        "esf,efd->esd",
-        lax.all_gather(hidden, "gy", axis=1, tiled=True),
-        w_down,
-        preferred_element_type=jnp.float32,
+        "esf,efd->esd", note_islands_all(hidden, "gy"), w_down, preferred_element_type=jnp.float32
     )
     returned = lax.all_to_all(
         expert_out.astype(jnp.bfloat16), "gx", split_axis=1, concat_axis=0, tiled=True

time: 286 us -> 280 us (0.979)
  waiting for transfers between devices: 83.7 us -> 73.5 us
  starting transfers between devices: 7.49 us -> 11.6 us
    all_gather x1 -> x0, waiting for transfers between devices: 30.1 us -> none  [body(): lax.all_gather(hidden, 'gy', axis=1, tiled=True)]
    ppermute x0 -> x3, waiting for transfers between devices: none -> 19.9 us  [the longest x2 17.8 us: note_islands_all(): lax.ppermute(block_out[-1], axis_name=mesh_dim, perm=fields)]
    ppermute x0 -> x3, starting transfers between devices: none -> 4.42 us  [the longest x1 3.82 us: note_islands_all(): kept_arr.append(lax.ppermute(kept_arr[-1], axis_name=mesh_dim, perm=cards))]
    unnamed x4 -> x3, waiting for transfers between devices: 32.9 us -> 32.9 us
  transfers between devices with their start and end apart: 5 -> 7, of which waited for: 4 -> 6; matrix products, arithmetic and copies ran while one was open for 17% -> 17% of each run, Pallas kernels for 0% -> 0%
where the time goes in v1:
time: 280 us; the launch traced here: 279 us
  waiting for transfers between devices  73.5 us (26%)
  blocking collectives  63 us (22%)
  other arithmetic  45.7 us (16%)
  local copies, waits for them, and re-layouts  39.5 us (14%)
  matrix products  29.2 us (10%)
  between operations  16.1 us (6%)
  starting transfers between devices  11.6 us (4%)
    unnamed x3, waiting for transfers between devices  32.9 us
    all_gather x2, blocking collectives, combined_all(): lax.all_gather(a.astype(kind), axis)  32 us
    all_gather x1, blocking collectives, body(): qkv_whole = lax.all_gather(qkv_part, 'gy', axis=1, tiled=True)  19.6 us
    ppermute x2, waiting for transfers between devices, note_islands_all(): lax.ppermute(block_out[-1], axis_name=mesh_dim, perm=fields)  17.8 us
    scatter x1, local copies, waits for them, and re-layouts, body(): slot_table = jnp.full((expert_count * most_rows,), tok_rows, jnp.int32).a...  15.5 us
    another operation x1, other arithmetic, body(): slot_rank = jnp.cumsum(hit_count, 0) - 1  15.4 us
    all_to_all x1, waiting for transfers between devices, body(): lax.all_to_all(outgoing, 'gx', split_axis=0, concat_axis=1, tiled=True)  15.3 us
    unnamed x1, blocking collectives  11.3 us
  transfers between devices with their start and end apart: 7, of which 6 were waited for; matrix products, arithmetic and copies ran while one was open for 17% of the time, Pallas kernels for 0%

profile of v1, /device:TPU:0, one launch (start us, length us, event | category | flops | bytes accessed | tf_op | source)
XLA Modules:
  0.0 278.9 jit_solution(16132391632648228486)
XLA Ops:
  7.2 0.7 convert_element_type.348
  7.9 1.1 fusion.38
  9.1 3.7 %convolution_convert_fusion.1 = bf16[64,1280]{1,0:T(8,128)(2,1)S(1)} fusion(bf16[2048,1280]{1,0:T(8,128)(2,1)} %param.20, bf16[64,2048]{1,0:T(8,128)(2,1)} %param.18, f32[2048]{0:T(1024)S(1)} %convert_element_type.348, f32[64]{0:T(128)S(1)} %add_rsqrt_fusion.3), kind=kOutput, calls=%fused_computation.23 | convolution fusion | flops 336150528 | bytes 5677312 | tf_op jit(solution)/shard_map/dot_general | solution.py:92
  12.7 19.6 %all_gather.17 = bf16[64,5120]{1,0:T(8,128)(2,1)S(1)} all-gather(bf16[64,1280]{1,0:T(8,128)(2,1)S(1)} %convolution_convert_fusion.1), channel_id=1, replica_groups=mesh['gx'=8,'gy'=4] {'gy'}, dimensions={1}, use_global_device_ids=true | all-gather | bytes 819200 | tf_op jit(solution)/shard_map/all_gather | solution.py:93
  32.5 0.7 slice_bitcast_fusion.2
  34.0 0.4 multiply_reduce_fusion.1
  34.8 0.3 reshape.690
  35.1 0.3 fusion.33
  35.6 0.4 fusion.41
  36.1 0.3 pad_maximum_fusion
  36.4 4.7 %fusion.6 = (f32[64,4,8]{2,0,1:T(8,128)S(1)}, f32[4,64,8,1024]{3,2,1,0:T(8,128)}) fusion(pred[1024]{0:T(1024)(128)(4,1)S(1)} %add_compare_fusion, bf16[64,4,8,128]{3,2,0,1:T(8,128)(2,1)S(1)} %pad_maximum_fusion, bf16[1024,4,128,1]{2,1,0,3:T(4,128)(2,1)S(1)} %bitcast.183), kind=kOutput, calls=%fused_computation.18 | convolution fusion | flops 543160320 | bytes 9970688 | tf_op jit(solution)/shard_map/rtkgd,rskd->rtkgs/dot_general | solution.py:114
  41.8 0.7 fusion.75
  42.6 0.3 fusion.59
  42.9 0.3 copy.246
  43.3 0.3 reshape.692
  43.6 0.3 fusion.57
  43.9 5.5 %fusion.24 = bf16[1,64,4,8,128]{4,3,1,2,0:T(8,128)(2,1)S(1)} fusion(f32[4,128,64,8]{1,3,2,0:T(8,128)S(1)} %fusion.57, bf16[1024,4,128,1]{2,1,0,3:T(4,128)(2,1)S(1)} %bitcast.188, f32[4,64,8,1024]{3,2,1,0:T(8,128)} %get-tuple-element.264, f32[64,4,8]{2,0,1:T(8,128)S(1)} %copy.215, pred[1024]{0:T(1024)(128)(4,1)S(1)} %add_compare_fusion), kind=kOutput, calls=%fused_computation.38 | convolution fusion | flops 547880960 | bytes 11019264 | tf_op jit(solution)/shard_map/rtkgs,rskd->rtkgd/dot_general | solution.py:136
  49.4 0.9 copy.222
  50.7 0.7 copy.232
  51.4 15.4 %fusion.79 = s32[64,64,1]{2,1,0:T(8,128)S(1)} fusion(s32[64,64,1]{2,1,0:T(8,128)S(1)} %copy.232), kind=kOutput, calls=%fused_computation.151 | output fusion | flops 258048 | bytes 32768 | tf_op jit(solution)/shard_map/jit(cumsum)/reduce_window_sum | solution.py:159
  66.8 1.2 fusion.9
  68.3 16.1 %all-gather = bf16[256,4,8]{2,1,0:T(4,128)(2,1)S(1)} all-gather(bf16[64,4,8]{2,1,0:T(4,128)(2,1)S(1)} %copy.214), channel_id=2, replica_groups=mesh['gx'=8,'gy'=4] {'gy'}, dimensions={0}, use_global_device_ids=true | all-gather | bytes 20480 | tf_op jit(solution)/shard_map/all_gather | solution.py:14
  84.6 4.7 %convert_reduce_fusion = f32[64,4,8]{2,0,1:T(8,128)S(1)} fusion(f32[64,4,8]{2,0,1:T(8,128)S(1)} %copy.215, f32[4,64,8,1024]{3,2,1,0:T(8,128)} %get-tuple-element.264, pred[1024]{0:T(1024)(128)(4,1)S(1)} %add_compare_fusion), kind=kLoop, calls=%fused_computation.16 | loop fusion | flops 14678016 | bytes 8406016 | tf_op jit(solution)/shard_map/reduce_sum | solution.py:133
  89.5 15.9 %all-gather.1 = bf16[256,4,8]{2,1,0:T(4,128)(2,1)S(1)} all-gather(bf16[64,4,8]{2,1,0:T(4,128)(2,1)S(1)} %copy.217), channel_id=3, replica_groups=mesh['gx'=8,'gy'=4] {'gy'}, dimensions={0}, use_global_device_ids=true | all-gather | bytes 20480 | tf_op jit(solution)/shard_map/all_gather | solution.py:14
  105.8 15.5 %scatter_custom_fusion = s32[768]{0:T(1024)S(1)} fusion(s32[4096]{0:T(1024)S(1)} %reshape.728, s32[4096]{0:T(1024)S(1)} %reshape.730, s32[]{:T(128)} %constant.142.clone.1), kind=kCustom, calls=%fused_computation.132 | custom fusion | bytes 3076 | tf_op jit(solution)/shard_map/scatter | solution.py:169
  121.3 1.2 slice_convert_fusion
  122.5 6.7 %while.19 = (s32[]{:T(128)}, f32[1,64,4,8]{1,3,2,0:T(8,128)S(1)}, f32[1,64,4,8]{1,3,2,0:T(8,128)S(1)}, f32[1,64,4,8,128]{4,3,2,1,0:T(8,128)S(1)}, bf16[4,1,64,4,...) while((s32[]{:T(128)}, f32[1,64,4,8]{1,3,2,0:T(8,128)S(1)}, ...), condition=%wide.region_9.10_spmd, body=%wide.region_8.9_spmd.sunk | while | flops 1069061 | bytes 2764955 | solution.py:26
  122.8 1.9 fusion.93
  125.1 1.9 fusion.93
  127.3 1.9 fusion.93
  129.4 0.3 divide_convert_fusion
  130.0 3.0 %fusion.28 = bf16[64,512]{1,0:T(8,128)(2,1)S(1)} fusion(bf16[64,4096]{1,0:T(8,128)(2,1)S(1)} %reshape.695, bf16[4096,512]{1,0:T(8,128)(2,1)} %param.27, bf16[64,2048]{1,0:T(8,128)(2,1)} %param.18, s32[]{:T(128)S(6)} %select_n.106), kind=kOutput, calls=%fused_computation.41 | convolution fusion | flops 268533760 | bytes 4849668 | tf_op jit(solution)/shard_map/dot_general | solution.py:146
  133.0 2.7 gather_fusion
  135.7 1.2 reshape.696
  136.9 3.6 %all-to-all-start = ((bf16[64,12,512]{2,1,0:T(8,128)(2,1)}), bf16[64,12,512]{2,1,0:T(8,128)(2,1)S(1)}, u32[]{:S(2)}, u32[]{:S(2)}) async-start(bf16[64,12,512]{2,1,0:T(8,128)(2,1)} %reshape.696), calls=%async_computation | async-start | bytes 2097152 | tf_op jit(solution)/shard_map/all_to_all | solution.py:173
  140.6 15.3 %all-to-all-done = bf16[64,12,512]{2,1,0:T(8,128)(2,1)S(1)} async-done(((bf16[64,12,512]{2,1,0:T(8,128)(2,1)}), bf16[64,12,512]{2,1,0:T(8,128)(2,1)S(1)}, u32[]{:S(2)}, u32[]{:S(2)}) %all-to-all-start) | async-done | bytes 786464 | tf_op jit(solution)/shard_map/all_to_all | solution.py:173
  155.9 0.5 copy.234
  156.6 6.7 %fusion.76 = bf16[12,8,8,1536]{3,1,0,2:T(8,128)(2,1)S(1)} fusion(bf16[8,512,1536]{2,1,0:T(8,128)(2,1)} %param.31, bf16[8,96,512]{2,0,1:T(8,128)(2,1)S(1)} %fusion.10), kind=kOutput, calls=%fused_computation.150 | convolution fusion | flops 1209139200 | bytes 15728640 | tf_op jit(solution)/shard_map/esd,edf->esf/dot_general | solution.py:177
  163.3 1.7 copy.265
  165.0 0.6 copy-done.10
  165.6 0.6 dynamic-slice
  166.9 0.3 multiply_reduce_fusion
  167.6 11.3 %all-reduce.2 = bf16[8,96]{1,0:T(8,128)(2,1)S(1)} all-reduce(bf16[8,96]{1,0:T(8,128)(2,1)S(1)} %convert_element_type.390), channel_id=6, replica_groups=mesh['gx'=8,'gy'=4] {'gy'}, use_global_device_ids=true, to_apply=%region_15.16.clone | all-reduce | flops 768 | bytes 3072
  179.0 32.8 %reduce-scatter.5.cloned.1.call-done = bf16[24,12288]{1,0:T(8,128)(2,1)} async-done(((bf16[96,12288]{1,0:T(8,128)(2,1)}), bf16[24,12288]{1,0:T(8,128)(2,1)}) %reduce-scatter.5.cloned.1.call-update) | async-done | bytes 589840
  211.9 1.2 copy.266
  213.3 0.2 fusion.37
  213.6 0.6 collective-permute-start
  214.2 9.9 %collective-permute-done = bf16[8,24,768]{2,1,0:T(8,128)(2,1)S(1)} collective-permute-done((bf16[8,24,768]{2,1,0:T(8,128)(2,1)S(1)}, bf16[8,24,768]{2,1,0:T(8,128)(2,1)S(1)}, u32[]{:S(2)}, u32[]{:S(2)}) %collective-permute-start) | collective-permute-done | bytes 294944 | tf_op jit(solution)/shard_map/ppermute | solution.py:197
  224.1 3.8 %collective-permute-start.2 = (bf16[8,24,768]{2,1,0:T(8,128)(2,1)S(1)}, bf16[8,24,768]{2,1,0:T(8,128)(2,1)S(1)}, u32[]{:S(2)}, u32[]{:S(2)}) collective-permute-start(bf16[8,24,768]{2,1,0:T(8,128)(2,1)S(1)} %fusion.37), channel_id=1, source_target_pairs={{0,3},{1,0},{2,1},{3,2},{4,7},{5,4},{6,5},{7,6},{8,11},{9,8},{10,9... | collective-permute-start | bytes 884744 | tf_op jit(solution)/shard_map/ppermute | solution.py:199
  227.9 7.9 %collective-permute-done.1 = bf16[8,24,768]{2,1,0:T(8,128)(2,1)S(1)} collective-permute-done((bf16[8,24,768]{2,1,0:T(8,128)(2,1)S(1)}, bf16[8,24,768]{2,1,0:T(8,128)(2,1)S(1)}, u32[]{:S(2)}, u32[]{:S(2)}) %collective-permute-start.1) | collective-permute-done | bytes 294944 | tf_op jit(solution)/shard_map/ppermute | solution.py:197
  235.9 0.2 constant_dynamic-update-slice_fusion.5
  236.1 2.1 collective-permute-done.2
  238.3 0.2 constant_dynamic-update-slice_fusion.1
  238.5 4.0 %convolution_convert_fusion.2 = bf16[8,96,512]{2,1,0:T(8,128)(2,1)S(1)} fusion(bf16[8,768,512]{2,1,0:T(8,128)(2,1)} %param.32, bf16[8,192,768]{2,1,0:T(8,128)(2,1)S(1)} %constant_dynamic-update-slice_fusion, s32[]{:T(128)S(6)} %select_n.117), kind=kOutput, calls=%fused_computation.31 | convolution fusion | flops 604372992 | bytes 8257540 | tf_op jit(solution)/shard_map/esf,efd->esd/dot_general | solution.py:204
  242.5 1.3 copy.238
  243.8 3.5 %all-to-all-start.1 = ((bf16[8,96,512]{2,0,1:T(8,128)(2,1)}), bf16[8,96,512]{2,0,1:T(8,128)(2,1)S(1)}, u32[]{:S(2)}, u32[]{:S(2)}) async-start(bf16[8,96,512]{2,0,1:T(8,128)(2,1)} %copy.238), calls=%async_computation.1 | async-start | bytes 1572864 | tf_op jit(solution)/shard_map/all_to_all | solution.py:207
  247.3 0.8 constant_dynamic-slice_fusion
  248.5 5.1 %gather_fusion.1 = f32[768]{0:T(1024)S(1)} fusion(f32[65,64]{1,0:T(8,128)S(1)} %concatenate.52, s32[768]{0:T(1024)S(1)} %fusion.63), kind=kCustom, calls=%fused_computation.1 | custom fusion | bytes 12288 | tf_op jit(solution)/shard_map/gather | solution.py:212
  253.8 0.7 fusion.29
  254.5 5.4 %all-to-all-done.1 = bf16[8,96,512]{2,0,1:T(8,128)(2,1)S(1)} async-done(((bf16[8,96,512]{2,0,1:T(8,128)(2,1)}), bf16[8,96,512]{2,0,1:T(8,128)(2,1)S(1)}, u32[]{:S(2)}, u32[]{:S(2)}) %all-to-all-start.1) | async-done | bytes 786464 | tf_op jit(solution)/shard_map/all_to_all | solution.py:207
  260.1 0.9 copy.239
  261.0 1.3 reshape.709
  262.4 9.0 %scatter_custom_fusion.1 = f32[65,512]{1,0:T(8,128)S(1)} fusion(s32[768]{0:T(1024)S(1)} %get-tuple-element.260, f32[768,512]{1,0:T(8,128)} %reshape.709, f32[768]{0:T(1024)S(1)} %gather_fusion.1, f32[]{:T(128)} %constant.132.clone.1), kind=kCustom, calls=%fused_computation.29 | custom fusion | flops 786432 | bytes 1710084 | tf_op jit(solution)/shard_map/scatter-add | solution.py:216
  271.4 0.6 fusion.48
  (110 shorter events, 5.9 us)
Async XLA Ops:
  7.2 43.1 %copy-start = (s32[512,8]{0,1:T(8,128)S(1)}, s32[512,8]{0,1:T(8,128)}, u32[]{:S(2)}) copy-start(s32[512,8]{0,1:T(8,128)} %param.29) | copy-start | bytes 49156
  7.2 114.2 %all-gather.5.cloned.1.call-start = ((), (), s32[]{:S(2)}) async-start(), calls=%async_computation.3 | async-start | bytes 2621440 | tf_op jit(solution)/shard_map/all_gather | solution.py:14
  12.7 21.2 %copy-start.8 = (bf16[128]{0:T(256)(128)(2,1)S(1)}, bf16[128]{0:T(256)(128)(2,1)}, u32[]{:S(2)}) copy-start(bf16[128]{0:T(256)(128)(2,1)} %param.21) | copy-start | bytes 772
  32.4 2.2 copy-start.4
  32.4 2.3 copy-start.2
  36.4 4.8 %copy-start.9 = (bf16[128]{0:T(256)(128)(2,1)S(1)}, bf16[128]{0:T(256)(128)(2,1)}, u32[]{:S(2)}) copy-start(bf16[128]{0:T(256)(128)(2,1)} %param.22) | copy-start | bytes 772
  41.8 1.4 copy-start.3
  135.7 4.8 %copy-start.6 = (bf16[512]{0:T(512)(128)(2,1)S(1)}, bf16[512]{0:T(512)(128)(2,1)}, u32[]{:S(2)}) copy-start(bf16[512]{0:T(512)(128)(2,1)} %param.28) | copy-start | bytes 3076
  136.9 19.0 %all-to-all-start = ((bf16[64,12,512]{2,1,0:T(8,128)(2,1)}), bf16[64,12,512]{2,1,0:T(8,128)(2,1)S(1)}, u32[]{:S(2)}, u32[]{:S(2)}) async-start(bf16[64,12,512]{2,1,0:T(8,128)(2,1)} %reshape.696), calls=%async_computation | async-start | bytes 2097152 | tf_op jit(solution)/shard_map/all_to_all | solution.py:173
  140.5 71.4 %reduce-scatter.5.cloned.1.call-start = ((), (), s32[]{:S(2)}) async-start(), calls=%async_computation.4 | async-start | bytes 2949120
  165.0 0.7 copy-start.10
  213.6 10.5 %collective-permute-start = (bf16[8,24,768]{2,1,0:T(8,128)(2,1)S(1)}, bf16[8,24,768]{2,1,0:T(8,128)(2,1)S(1)}, u32[]{:S(2)}, u32[]{:S(2)}) collective-permute-start(bf16[8,24,768]{2,1,0:T(8,128)(2,1)S(1)} %fusion.37), channel_id=1, source_target_pairs={{0,1},{1,2},{2,3},{3,0},{4,5},{5,6},{6,7},{7,4},{8,9},{9,10},{10,1... | collective-permute-start | bytes 884744 | tf_op jit(solution)/shard_map/ppermute | solution.py:197
  224.1 11.7 %collective-permute-start.1 = (bf16[8,24,768]{2,1,0:T(8,128)(2,1)S(1)}, bf16[8,24,768]{2,1,0:T(8,128)(2,1)S(1)}, u32[]{:S(2)}, u32[]{:S(2)}) collective-permute-start(bf16[8,24,768]{2,1,0:T(8,128)(2,1)S(1)} %collective-permute-done), channel_id=1, source_target_pairs={{0,1},{1,2},{2,3},{3,0},{4,5},{5,6},{6,7},{7,4},{8,9},{9,10},{10,1... | collective-permute-start | bytes 884744 | tf_op jit(solution)/shard_map/ppermute | solution.py:197
  224.1 14.1 %collective-permute-start.2 = (bf16[8,24,768]{2,1,0:T(8,128)(2,1)S(1)}, bf16[8,24,768]{2,1,0:T(8,128)(2,1)S(1)}, u32[]{:S(2)}, u32[]{:S(2)}) collective-permute-start(bf16[8,24,768]{2,1,0:T(8,128)(2,1)S(1)} %fusion.37), channel_id=1, source_target_pairs={{0,3},{1,0},{2,1},{3,2},{4,7},{5,4},{6,5},{7,6},{8,11},{9,8},{10,9... | collective-permute-start | bytes 884744 | tf_op jit(solution)/shard_map/ppermute | solution.py:199
  243.8 16.1 %all-to-all-start.1 = ((bf16[8,96,512]{2,0,1:T(8,128)(2,1)}), bf16[8,96,512]{2,0,1:T(8,128)(2,1)S(1)}, u32[]{:S(2)}, u32[]{:S(2)}) async-start(bf16[8,96,512]{2,0,1:T(8,128)(2,1)} %copy.238), calls=%async_computation.1 | async-start | bytes 1572864 | tf_op jit(solution)/shard_map/all_to_all | solution.py:207
  248.5 5.3 %copy-start.5 = (bf16[1,64,512]{2,1,0:T(8,128)(2,1)S(1)}, bf16[1,64,512]{2,1,0:T(8,128)(2,1)}, u32[]{:S(2)}) copy-start(bf16[1,64,512]{2,1,0:T(8,128)(2,1)} %get-tuple-element.254) | copy-start | bytes 196612
  248.5 5.3 %copy-start.7 = (s32[1,8,64]{2,1,0:T(8,128)S(1)}, s32[1,8,64]{2,1,0:T(8,128)}, u32[]{:S(2)}) copy-start(s32[1,8,64]{2,1,0:T(8,128)} %param.33) | copy-start | bytes 6148
  260.1 11.9 %copy-start.1 = (s32[512,8]{0,1:T(8,128)S(1)}, s32[512,8]{0,1:T(8,128)}, u32[]{:S(2)}) copy-start(s32[512,8]{0,1:T(8,128)} %param.29) | copy-start | bytes 49156
Sparse Core Ops, SparseCore 0:
  50.4 54.0 all-gather.4
  165.1 46.7 reduce-scatter.4
